TPU v7x, 32 devices: a whole 2x2x4 slice. The times are simulated.
32 devices in a mesh: section: 2 (over x), dp: 4 (over z), mp: 4 (over y, core).
Axes of the slice: x: 2, y: 2, z: 4, core: 2. Of those that a mesh axis runs over, the one named last changes fastest.
Arguments:
- w_query: bfloat16 [2, 4096, 4096], P('section', None, 'mp'), may hold values from -0.09375 to 0.09375
- w_key: bfloat16 [2, 4096, 1024], P('section', None, 'mp'), may hold values from -0.09375 to 0.09375
- w_value: bfloat16 [2, 4096, 1024], P('section', None, 'mp'), may hold values from -0.09375 to 0.09375
- w_out: bfloat16 [2, 4096, 4096], P('section', 'mp'), may hold values from -0.09375 to 0.09375
- norm_gain: bfloat16 [2, 4096], P('section', 'mp'), may hold values from 0.099609375 to 1.8984375
- saved_input: bfloat16 [2, 2, 4, 64, 4096], P('section', None, 'dp', None, 'mp'), may hold values from -6 to 6
- saved_query: bfloat16 [2, 2, 4, 64, 4096], P('section', None, 'dp', None, 'mp'), may hold values from -5 to 5
- saved_key: bfloat16 [2, 2, 4, 64, 1024], P('section', None, 'dp', None, 'mp'), may hold values from -5 to 5
- saved_value: bfloat16 [2, 2, 4, 64, 1024], P('section', None, 'dp', None, 'mp'), may hold values from -6 to 6
- grad_in: bfloat16 [2, 4, 64, 4096], P('section', 'dp', None, 'mp'), may hold values from -0.29882812 to 0.29882812
- fresh_grad: bfloat16 [1, 4, 64, 4096], P(None, 'dp', None, 'mp'), may hold values from -0.29882812 to 0.29882812
- features: bfloat16 [2, 4, 16, 7680], P(None, 'dp', None, 'section'), may hold values from -6 to 6
- image_pos: int32 [2, 4, 16], P(None, 'dp'), may hold values from 0 to 63, as said below
Outputs:
- proj_grad: bfloat16 [7680, 4096], P(('section', 'dp'), 'mp')
- pending: bfloat16 [2, 4, 64, 4096], P('section', 'dp', None, 'mp')
Inputs may be any that keep to these rules, and one draw needn't show every extreme that they name: `image_pos`: each row holds 16 consecutive ascending positions; the first row starts at 0 and the last ends at 63.
All inputs are finite; a program needn't handle non-finite values.
Results may differ from a plain program's by a relative error of at most 0.017.
Values may be sent and summed in bfloat16 or wider, within the bound.
A program may use at most 64 MiB of HBM per device.

v0:
```python
import jax
import jax.numpy as jnp
from jax import lax
from jax.sharding import PartitionSpec as P

D = 4096
HD = 128
TICKS = 2


def shifted(block, axis, distance):
    devices = range(lax.axis_size(axis))
    route = [(i - distance, i) for i in devices if i - distance in devices]
    return lax.ppermute(block, axis, route)


def spread_2(block, axis, holder):
    block = jnp.where(lax.axis_index(axis) == holder, block, jnp.zeros_like(block))
    return lax.psum(block, axis)


def attention_back(query, key_in, value, d_attn):
    seq_len = query.shape[0]
    kv_local = key_in.shape[1] // HD
    group = query.shape[1] // key_in.shape[1]
    scale = HD ** (-0.5)
    q_four = query.reshape(seq_len, kv_local, group, HD)
    k_three = key_in.reshape(seq_len, kv_local, HD)
    v_three = value.reshape(seq_len, kv_local, HD)
    a_four = d_attn.reshape(seq_len, kv_local, group, HD)
    scores = (
        jnp.einsum("lgjd,mgd->gjlm", q_four, k_three, preferred_element_type=jnp.float32) * scale
    )
    rows = jnp.arange(seq_len)[:, None]
    cols = jnp.arange(seq_len)[None, :]
    scores = jnp.where(cols <= rows, scores, -1e30)
    top = jnp.max(scores, -1, keepdims=True)
    expo = jnp.exp(scores - top)
    probs = expo / jnp.sum(expo, -1, keepdims=True)
    d_probs = jnp.einsum("lgjd,mgd->gjlm", a_four, v_three, preferred_element_type=jnp.float32)
    inner = jnp.sum(probs * d_probs, -1, keepdims=True)
    d_scores = (probs * (d_probs - inner) * scale).astype(jnp.bfloat16)
    probs_half = probs.astype(jnp.bfloat16)
    d_query = jnp.einsum(
        "gjlm,mgd->lgjd", d_scores, k_three, preferred_element_type=jnp.float32
    ).astype(jnp.bfloat16)
    d_key = jnp.einsum(
        "gjlm,lgjd->mgd", d_scores, q_four, preferred_element_type=jnp.float32
    ).astype(jnp.bfloat16)
    d_value = jnp.einsum(
        "gjlm,lgjd->mgd", probs_half, a_four, preferred_element_type=jnp.float32
    ).astype(jnp.bfloat16)
    return (d_query.reshape(seq_len, -1), d_key.reshape(seq_len, -1), d_value.reshape(seq_len, -1))


def segment_step(grad, x_saved, gain, w_q, w_k, w_v, w_o, query, key_in, value):
    x_float = x_saved.astype(jnp.float32)
    squares_local = jnp.sum(x_float * x_float, -1)
    d_attn = lax.dot_general(
        lax.all_gather(grad, "mp", axis=1, tiled=True),
        w_o,
        (((1,), (1,)), ((), ())),
        preferred_element_type=jnp.float32,
    ).astype(jnp.bfloat16)
    d_query, d_key, d_value = attention_back(query, key_in, value, d_attn)
    contract = (((1,), (1,)), ((), ()))
    partial_term = lax.dot_general(d_query, w_q, contract, preferred_element_type=jnp.float32)
    partial_term = partial_term + lax.dot_general(
        d_key, w_k, contract, preferred_element_type=jnp.float32
    )
    partial_term = partial_term + lax.dot_general(
        d_value, w_v, contract, preferred_element_type=jnp.float32
    )
    d_normed = lax.psum_scatter(
        partial_term.astype(jnp.bfloat16), "mp", scatter_dimension=1, tiled=True
    ).astype(jnp.float32)
    weighted = gain.astype(jnp.float32) * d_normed
    cross_local = jnp.sum(x_float * weighted, -1)
    squares, cross = lax.psum((squares_local, cross_local), "mp")
    rstd = lax.rsqrt(squares / D + 1e-05)[:, None]
    d_input = rstd * weighted - x_float * rstd**3 * (cross / D)[:, None]
    return (grad.astype(jnp.float32) + d_input).astype(jnp.bfloat16)


def shards(
    w_query,
    w_key,
    w_value,
    w_out,
    norm_gain,
    saved_input,
    saved_query,
    saved_key,
    saved_value,
    grad_in,
    fresh_grad,
    features,
    image_pos,
):
    segments = lax.axis_size("section")
    here = lax.axis_index("section")
    held = grad_in[0, 0]
    picks = []
    produced = held
    for tick in range(TICKS):
        produced = segment_step(
            held,
            saved_input[0, tick, 0],
            norm_gain[0],
            w_query[0],
            w_key[0],
            w_value[0],
            w_out[0],
            saved_query[0, tick, 0],
            saved_key[0, tick, 0],
            saved_value[0, tick, 0],
        )
        picks.append(jnp.take(produced, image_pos[tick, 0], axis=0))
        if tick + 1 < TICKS:
            moved = shifted(produced, "section", -1)
            held = jnp.where(here == segments - 1, fresh_grad[tick, 0], moved)
    image_grad = spread_2(jnp.stack(picks), "section", 0)
    spread = lax.all_to_all(features, "dp", split_axis=3, concat_axis=1, tiled=True)
    total = jnp.einsum(
        "knif,knid->fd",
        spread,
        lax.all_gather(image_grad[:, None], "dp", axis=1, tiled=True),
        preferred_element_type=jnp.float32,
    )
    return (total.astype(jnp.bfloat16), produced[None, None])


def solution(mesh):
    in_specs = (
        P("section", None, "mp"),
        P("section", None, "mp"),
        P("section", None, "mp"),
        P("section", "mp", None),
        P("section", "mp"),
        P("section", None, "dp", None, "mp"),
        P("section", None, "dp", None, "mp"),
        P("section", None, "dp", None, "mp"),
        P("section", None, "dp", None, "mp"),
        P("section", "dp", None, "mp"),
        P(None, "dp", None, "mp"),
        P(None, "dp", None, "section"),
        P(None, "dp", None),
    )
    out_specs = (P(("section", "dp"), "mp"), P("section", "dp", None, "mp"))
    return jax.shard_map(shards, mesh=mesh, in_specs=in_specs, out_specs=out_specs, check_vma=False)
```

profile of v0, /device:TPU:2, one launch (start us, length us, event | category | flops | bytes accessed | tf_op | source)
XLA Modules:
  0.0 172.4 jit_solution(17616110696914920149)
XLA Ops:
  7.2 0.9 fusion.133
  8.2 0.8 fusion.134
  9.0 1.0 fusion.132
  10.1 7.4 %all-gather = bf16[1,1,64,4096]{3,2,1,0:T(8,128)(2,1)S(1)} all-gather(bf16[1,1,64,1024]{3,2,1,0:T(8,128)(2,1)} %param.24), channel_id=2, replica_groups=mesh['section'=2,'dp'=4,'mp'=4] {'mp'}, dimensions={3}, use_global_device_ids=true | all-gather | bytes 655360 | tf_op jit(solution)/shard_map/all_gather | solution.py:60
  17.5 6.0 %fusion.35 = bf16[64,1024]{1,0:T(8,128)(2,1)S(1)} fusion(bf16[1,1024,4096]{2,1,0:T(8,128)(2,1)} %param.18, bf16[1,1,64,4096]{3,2,1,0:T(8,128)(2,1)S(1)} %all-gather), kind=kOutput, calls=%fused_computation.46 | convolution fusion | flops 536936448 | bytes 9043968 | tf_op jit(solution)/shard_map/dot_general | solution.py:59
  23.6 0.2 convolution_bitcast_fusion.1
  23.8 0.3 fusion.135
  24.1 0.2 fusion.48
  24.4 0.2 fusion.50
  24.6 0.3 fusion.41
  24.9 0.1 copy.75
  25.1 6.0 %fusion.6 = f32[64,4096]{1,0:T(8,128)S(1)} fusion(bf16[64,1024]{1,0:T(8,128)(2,1)S(1)} %reshape.54, bf16[1,4096,1024]{2,1,0:T(8,128)(2,1)} %param.15), kind=kOutput, calls=%fused_computation.8 | convolution fusion | flops 536870912 | bytes 9568256 | tf_op jit(solution)/shard_map/dot_general | solution.py:67
  31.1 0.8 convolution_add_fusion.3
  31.9 0.8 copy-done.1
  32.7 1.6 fusion.12
  34.5 22.4 %reduce-scatter.3.cloned.1.call-done = bf16[64,1024]{1,0:T(8,128)(2,1)} async-done(((bf16[64,4096]{1,0:T(8,128)(2,1)}), bf16[64,1024]{1,0:T(8,128)(2,1)}) %reduce-scatter.3.cloned.1.call-update) | async-done | bytes 131088 | tf_op jit(solution)/shard_map/reduce_scatter | solution.py:74
  56.9 1.1 fusion.66
  58.1 5.9 %all-reduce.1 = (f32[64]{0:T(128)S(1)}, f32[64]{0:T(128)S(1)}) all-reduce(f32[64]{0:T(128)S(1)} %get-tuple-element.4, f32[64]{0:T(128)S(1)} %get-tuple-element.5), channel_id=1, replica_groups=mesh['section'=2,'dp'=4,'mp'=4] {'mp'}, use_global_device_ids=true, to_apply=%region_7.8 | all-reduce | flops 128 | bytes 1024 | tf_op jit(solution)/shard_map/psum | solution.py:79
  64.0 1.0 fusion.64
  65.1 2.3 %collective-permute-start = (bf16[64,1024]{1,0:T(8,128)(2,1)S(1)}, bf16[64,1024]{1,0:T(8,128)(2,1)S(1)}, u32[]{:S(2)}, u32[]{:S(2)}) collective-permute-start(bf16[64,1024]{1,0:T(8,128)(2,1)S(1)} %fusion.64), channel_id=1, source_target_pairs={{16,0},{17,1},{18,2},{19,3},{20,4},{21,5},{22,6},{23,7},{24,8},{25... | collective-permute-start | bytes 393224 | tf_op jit(solution)/shard_map/ppermute | solution.py:14
  67.4 1.0 fusion.140
  68.3 1.7 collective-permute-done
  70.0 6.9 %all_gather.10 = bf16[64,4096]{1,0:T(8,128)(2,1)S(1)} all-gather(bf16[64,1024]{1,0:T(8,128)(2,1)S(1)} %bitcast_select_fusion), channel_id=1, replica_groups=mesh['section'=2,'dp'=4,'mp'=4] {'mp'}, dimensions={1}, use_global_device_ids=true | all-gather | bytes 655360 | tf_op jit(solution)/shard_map/all_gather | solution.py:60
  77.0 6.0 %fusion.38 = bf16[64,1024]{1,0:T(8,128)(2,1)S(1)} fusion(bf16[64,4096]{1,0:T(8,128)(2,1)S(1)} %all_gather.10, bf16[1,1024,4096]{2,1,0:T(8,128)(2,1)} %param.18), kind=kOutput, calls=%fused_computation.47 | convolution fusion | flops 536936448 | bytes 9043968 | tf_op jit(solution)/shard_map/dot_general | solution.py:59
  83.1 0.2 convolution_bitcast_fusion
  83.3 1.2 fusion.47
  84.5 1.3 fusion.49
  85.8 1.3 fusion.42
  87.1 0.1 copy.86
  87.3 6.0 %fusion.4 = f32[64,4096]{1,0:T(8,128)S(1)} fusion(bf16[64,1024]{1,0:T(8,128)(2,1)S(1)} %reshape.58, bf16[1,4096,1024]{2,1,0:T(8,128)(2,1)} %param.15), kind=kOutput, calls=%fused_computation.6 | convolution fusion | flops 536870912 | bytes 9568256 | tf_op jit(solution)/shard_map/dot_general | solution.py:67
  93.3 0.8 convolution_add_fusion.1
  94.1 0.8 copy-done.2
  94.9 1.6 fusion.13
  96.5 3.1 %copy.91 = bf16[2,1,16,3840]{2,0,1,3:T(2,128)(2,1)} copy(bf16[2,1,16,3840]{3,2,1,0:T(8,128)(2,1)S(1)} %copy-done.6) | data formatting | bytes 491520 | tf_op args[11]
  99.6 3.9 %reshape.99 = bf16[4,2,15360]{2,1,0:T(2,128)(2,1)} reshape(bf16[3840,1,2,16]{3,2,1,0:T(2,128)(2,1)} %bitcast.175) | data formatting | bytes 491520
  103.5 4.6 %all-to-all-start = ((bf16[4,2,15360]{2,1,0:T(2,128)(2,1)}), bf16[4,2,15360]{2,1,0:T(2,128)(2,1)S(1)}, u32[]{:S(2)}, u32[]{:S(2)}) async-start(bf16[4,2,15360]{2,1,0:T(2,128)(2,1)} %reshape.99), calls=%async_computation.2 | async-start | bytes 491520 | tf_op jit(solution)/shard_map/all_to_all | solution.py:123
  108.1 0.6 gather_fusion
  108.8 10.9 %reduce-scatter.5.cloned.1.call-done = bf16[64,1024]{1,0:T(8,128)(2,1)} async-done(((bf16[64,4096]{1,0:T(8,128)(2,1)}), bf16[64,1024]{1,0:T(8,128)(2,1)}) %reduce-scatter.5.cloned.1.call-update) | async-done | bytes 131088 | tf_op jit(solution)/shard_map/reduce_scatter | solution.py:74
  119.7 1.0 fusion.71
  120.8 5.9 %all-reduce = (f32[64]{0:T(128)S(1)}, f32[64]{0:T(128)S(1)}) all-reduce(f32[64]{0:T(128)S(1)} %fusion.71, f32[64]{0:T(128)S(1)} %get-tuple-element.3), channel_id=1, replica_groups=mesh['section'=2,'dp'=4,'mp'=4] {'mp'}, use_global_device_ids=true, to_apply=%region_15.17 | all-reduce | flops 128 | bytes 1024 | tf_op jit(solution)/shard_map/psum | solution.py:79
  126.7 1.0 fusion.70
  127.8 0.6 gather_fusion.1
  128.5 0.6 fusion.87
  129.1 2.3 %reshape.100 = bf16[3840,1,2,16]{3,2,1,0:T(2,128)(2,1)} reshape(bf16[4,2,15360]{2,1,0:T(2,128)(2,1)S(1)} %all-to-all-done) | data formatting | bytes 491520
  131.4 4.5 %copy.93 = bf16[2,1,16,4,960]{4,2,3,0,1:T(8,128)(2,1)S(1)} copy(bf16[2,1,16,4,960]{2,0,4,3,1:T(2,128)(2,1)} %bitcast.174) | data formatting | bytes 491520 | tf_op jit(solution)/shard_map/all_to_all | solution.py:123
  135.9 13.5 %all-reduce.4.cloned.1.call-done = bf16[2,1,16,1024]{3,2,1,0:T(8,128)(2,1)} async-done(((bf16[2,1,16,1024]{3,2,1,0:T(8,128)(2,1)}), bf16[2,1,16,1024]{3,2,1,0:T(8,128)(2,1)}) %all-reduce.4.cloned.1.call-update) | async-done | bytes 65552 | tf_op jit(solution)/shard_map/psum | solution.py:19
  149.4 14.5 %all_gather.11 = bf16[2,4,16,1024]{3,2,1,0:T(8,128)(2,1)S(1)} all-gather(bf16[2,1,16,1024]{3,2,1,0:T(8,128)(2,1)} %all-reduce.4.cloned.1.call-done), channel_id=1, replica_groups=mesh['section'=2,'dp'=4,'mp'=4] {'dp'}, dimensions={1}, use_global_device_ids=true | all-gather | bytes 327680 | tf_op jit(solution)/shard_map/all_gather | solution.py:127
  163.9 2.0 %fusion.18 = bf16[960,1024]{1,0:T(8,128)(2,1)} fusion(bf16[2,4,16,1024]{3,2,1,0:T(8,128)(2,1)S(1)} %all_gather.11, bf16[2,1,16,4,960]{4,2,3,0,1:T(8,128)(2,1)S(1)} %copy.93), kind=kOutput, calls=%fused_computation.25 | convolution fusion | flops 252641280 | bytes 2473984 | tf_op jit(solution)/shard_map/knif,knid->fd/dot_general | solution.py:124
  (46 shorter events, 0.9 us)
Async XLA Ops:
  7.2 24.0 %copy-start = (bf16[1,4096,256]{2,1,0:T(8,128)(2,1)S(1)}, bf16[1,4096,256]{2,1,0:T(8,128)(2,1)}, u32[]{:S(2)}) copy-start(bf16[1,4096,256]{2,1,0:T(8,128)(2,1)} %param.16) | copy-start | bytes 6291460
  7.2 49.8 %reduce-scatter.3.cloned.1.call-start = ((), (), s32[]{:S(2)}) async-start(), calls=%async_computation.3 | async-start | bytes 655360 | tf_op jit(solution)/shard_map/reduce_scatter | solution.py:74
  31.1 1.6 copy-start.1
  32.7 1.6 copy-start.8
  32.7 24.2 %copy-start.3 = (bf16[1,2,1,64,1024]{4,3,2,1,0:T(8,128)(2,1)S(1)}, bf16[1,2,1,64,1024]{4,3,2,1,0:T(8,128)(2,1)}, u32[]{:S(2)}) copy-start(bf16[1,2,1,64,1024]{4,3,2,1,0:T(8,128)(2,1)} %param.20) | copy-start | bytes 786436
  32.7 31.3 %copy-start.5 = (bf16[1,1,64,1024]{3,2,1,0:T(8,128)(2,1)S(1)}, bf16[1,1,64,1024]{3,2,1,0:T(8,128)(2,1)}, u32[]{:S(2)}) copy-start(bf16[1,1,64,1024]{3,2,1,0:T(8,128)(2,1)} %param.24) | copy-start | bytes 393220
  34.3 35.7 %copy-start.7 = (bf16[1,1,64,1024]{3,2,1,0:T(8,128)(2,1)S(1)}, bf16[1,1,64,1024]{3,2,1,0:T(8,128)(2,1)}, u32[]{:S(2)}) copy-start(bf16[1,1,64,1024]{3,2,1,0:T(8,128)(2,1)} %param.25) | copy-start | bytes 393220
  34.3 85.4 %reduce-scatter.5.cloned.1.call-start = ((), (), s32[]{:S(2)}) async-start(), calls=%async_computation.4 | async-start | bytes 655360 | tf_op jit(solution)/shard_map/reduce_scatter | solution.py:74
  65.1 4.9 %collective-permute-start = (bf16[64,1024]{1,0:T(8,128)(2,1)S(1)}, bf16[64,1024]{1,0:T(8,128)(2,1)S(1)}, u32[]{:S(2)}, u32[]{:S(2)}) collective-permute-start(bf16[64,1024]{1,0:T(8,128)(2,1)S(1)} %fusion.64), channel_id=1, source_target_pairs={{16,0},{17,1},{18,2},{19,3},{20,4},{21,5},{22,6},{23,7},{24,8},{25... | collective-permute-start | bytes 393224 | tf_op jit(solution)/shard_map/ppermute | solution.py:14
  93.3 1.6 copy-start.2
  94.9 1.6 copy-start.6
  96.5 11.6 %copy-start.9 = (s32[2,1,16]{2,1,0:T(1,128)S(1)}, s32[2,1,16]{2,1,0:T(1,128)}, u32[]{:S(2)}) copy-start(s32[2,1,16]{2,1,0:T(1,128)} %param.27) | copy-start | bytes 388
  103.5 25.6 %all-to-all-start = ((bf16[4,2,15360]{2,1,0:T(2,128)(2,1)}), bf16[4,2,15360]{2,1,0:T(2,128)(2,1)S(1)}, u32[]{:S(2)}, u32[]{:S(2)}) async-start(bf16[4,2,15360]{2,1,0:T(2,128)(2,1)} %reshape.99), calls=%async_computation.2 | async-start | bytes 491520 | tf_op jit(solution)/shard_map/all_to_all | solution.py:123
  108.1 41.3 %all-reduce.4.cloned.1.call-start = ((), (), s32[]{:S(2)}) async-start(), calls=%async_computation.5 | async-start | bytes 131072 | tf_op jit(solution)/shard_map/psum | solution.py:19
  127.8 8.1 %copy-start.4 = (bf16[64,1024]{1,0:T(8,128)(2,1)}, bf16[64,1024]{1,0:T(8,128)(2,1)S(1)}, u32[]{:S(2)}) copy-start(bf16[64,1024]{1,0:T(8,128)(2,1)S(1)} %fusion.70) | copy-start | bytes 393220
Sparse Core Ops, SparseCore 0:
  34.4 22.4 reduce-scatter.2
  96.6 23.0 reduce-scatter.4
  129.2 20.0 all-reduce.3
where the time goes:
time: 176 us; the launch traced here: 172 us
  waiting for transfers between devices  48.6 us (28%)
  blocking collectives  40.7 us (23%)
  matrix products  37.1 us (21%)
  local copies, waits for them, and re-layouts  20 us (11%)
  between operations  14 us (8%)
  starting transfers between devices  6.94 us (4%)
  other arithmetic  5.13 us (3%)
    reduce_scatter x2, waiting for transfers between devices, segment_step(): lax.psum_scatter(partial_term.astype(jnp.bfloat16), 'mp', scatter_dimensi...  33.4 us
    all_gather x1, blocking collectives, shards(): lax.all_gather(image_grad[:, None], 'dp', axis=1, tiled=True)  14.5 us
    all_gather x2, blocking collectives, segment_step(): lax.all_gather(grad, 'mp', axis=1, tiled=True)  14.3 us
    psum x1, waiting for transfers between devices, spread_2(): return lax.psum(block, axis)  13.5 us
    dot_general x2, matrix products, segment_step(): lax.dot_general(lax.all_gather(grad, 'mp', axis=1, tiled=True), w_o, (((1...  12.1 us
    dot_general x2, matrix products, segment_step(): lax.dot_general(d_query, w_q, contract, preferred_element_type=jnp.float32)  12.1 us
    psum x2, blocking collectives, segment_step(): squares, cross = lax.psum((squares_local, cross_local), 'mp')  11.9 us
    unnamed x23, local copies, waits for them, and re-layouts  10.9 us
  transfers between devices with their start and end apart: 5, of which 4 were waited for; matrix products, arithmetic and copies ran while one was open for 11% of the time, Pallas kernels for 0%

commit v1 on v0

v1 whole, which is shorter than its diff:
```python
import functools

import jax
import jax.numpy as jnp
from jax import lax
from jax.experimental import pallas as pl
from jax.experimental.pallas import tpu as pltpu
from jax.sharding import PartitionSpec as P

HD = 128
LANES = 128
TICKS = 2
GAIN_ROWS = 16
MESH = pl.DeviceIdType.MESH
LAST = (((1,), (1,)), ((), ()))
FIRST = (((0,), (0,)), ((), ()))
PLAIN = (((1,), (0,)), ((), ()))


def mul(a, b, dims):
    return lax.dot_general(a, b, dims, preferred_element_type=jnp.float32)


def lane_sum(a):
    parts = [a[:, i : i + LANES] for i in range(0, a.shape[1], LANES)]
    return functools.reduce(lambda p, q: p + q, parts)


def kernel(
    n_section, n_dp, n_mp, pieces,
    wq, wk, wv, wo, gain, x, q, k, v, g_in, fresh, feat, pos,
    feat_all, picks, pending,
    wq_s, wk_s, wv_s, wo_s, gain_s, x_s, q_s, k_s, v_s, g_s, feat_s, cut_s, pos_s,
    probs_s, attn_s, dq_s, dk_s, dv_s, out_s, send_s, recv_s, cross_s, cross_r,
    load_sem, wo_sem, wq_sem, wk_sem, wv_sem,
    ag_send, ag_recv, xg_send, xg_recv, rs_send, rs_recv, cr_send, cr_recv,
    held_send, held_recv, ft_send, ft_recv, px_send, px_recv, pz_send, pz_recv,
):
    section = lax.axis_index("section")
    seq = lax.axis_index("dp")
    me = lax.axis_index("mp")
    y, core = me // 2, me % 2
    partner = 2 * y + (1 - core)
    across = 2 * (1 - y) + core
    diag = 2 * (1 - y) + (1 - core)
    length = g_in.shape[2]
    width = g_in.shape[3]
    depth = width * n_mp
    kv_local = k.shape[4] // HD
    group = q.shape[4] // k.shape[4]
    scale = HD ** (-0.5)
    f32, bf16 = jnp.float32, jnp.bfloat16

    def remote(src, dst, ssem, rsem, where):
        return pltpu.make_async_remote_copy(
            src_ref=src, dst_ref=dst, send_sem=ssem, recv_sem=rsem,
            device_id=where, device_id_type=MESH,
        )

    loads = {}

    def load(name, src, dst, sem):
        loads[name] = pltpu.make_async_copy(src, dst, sem)
        loads[name].start()

    load("g", g_in.at[0, 0], g_s.at[0, me], load_sem.at[0])
    load("x0", x.at[0, 0, 0], x_s.at[0, me, pl.ds(0, length)], load_sem.at[1])
    load("gain", gain, gain_s, load_sem.at[2])
    load("x1", x.at[0, 1, 0], x_s.at[1, me, pl.ds(0, length)], load_sem.at[3])
    load("q", q.at[0, :, 0], q_s, load_sem.at[4])
    load("k", k.at[0, :, 0], k_s, load_sem.at[5])
    load("v", v.at[0, :, 0], v_s, load_sem.at[6])
    load("feat", feat.at[:, 0], feat_s, load_sem.at[7])
    load("pos", pos.at[:, 0], pos_s, load_sem.at[8])
    order = (me, partner, across, diag)
    for i, b in enumerate(order):
        columns = pl.ds(pl.multiple_of(b * width, width), width)
        load(f"wo{i}", wo.at[0, :, columns], wo_s.at[b], wo_sem.at[i])
    for i, b in enumerate((diag, across, partner, me)):
        rows = pl.ds(pl.multiple_of(b * width, width), width)
        load(f"wk{i}", wk.at[0, rows], wk_s.at[b], wk_sem.at[i])
        load(f"wv{i}", wv.at[0, rows], wv_s.at[b], wv_sem.at[i])
        load(f"wq{i}", wq.at[0, rows], wq_s.at[b], wq_sem.at[i])

    barrier = pltpu.get_barrier_semaphore()
    for b in (partner, across, diag):
        pl.semaphore_signal(barrier, inc=1, device_id={"mp": b}, device_id_type=MESH)
    for o in range(1, n_dp):
        pl.semaphore_signal(
            barrier, inc=1, device_id={"dp": (seq + o) % n_dp}, device_id_type=MESH
        )
    for o in range(1, n_section):
        pl.semaphore_signal(
            barrier, inc=1, device_id={"section": (section + o) % n_section}, device_id_type=MESH
        )
    pl.semaphore_wait(barrier, 3 + n_dp - 1 + n_section - 1)

    def gather_copy(buf, slot, rows, ssem, rsem, where):
        ref = buf.at[slot, rows]
        return remote(ref, ref, ssem, rsem, {"mp": where})

    def gather_start(buf, rows, ssem, rsem):
        gather_copy(buf, me, rows, ssem.at[1], rsem.at[1], across).start()
        gather_copy(buf, me, rows, ssem.at[0], rsem.at[0], partner).start()

    def gather_forward(buf, rows, ssem, rsem):
        gather_copy(buf, across, rows, ssem.at[1], rsem.at[1], across).wait_recv()
        gather_copy(buf, across, rows, ssem.at[2], rsem.at[2], partner).start()

    def gather_wait(buf, slot, which, rows, ssem, rsem):
        gather_copy(buf, slot, rows, ssem.at[which], rsem.at[which], partner).wait_recv()

    def gather_drain(buf, rows, ssem, rsem):
        for i in range(3):
            gather_copy(buf, me, rows, ssem.at[i], rsem.at[i], partner).wait_send()

    full = pl.ds(0, length)
    x_rows = (pl.ds(0, length + GAIN_ROWS), pl.ds(0, length))
    loads["g"].wait()
    gather_start(g_s.at[0], full, ag_send.at[0, 0], ag_recv.at[0, 0])
    loads["x0"].wait()
    loads["gain"].wait()
    x_s[0, me, pl.ds(length, GAIN_ROWS), :] = jnp.broadcast_to(
        gain_s[...], (GAIN_ROWS, width)
    )
    gather_start(x_s.at[0], x_rows[0], xg_send.at[0], xg_recv.at[0])
    loads["x1"].wait()
    gather_start(x_s.at[1], x_rows[1], xg_send.at[1], xg_recv.at[1])

    loads["feat"].wait()
    own_rows = feat_s.shape[2] // n_dp
    for j in range(n_dp):
        for t in range(TICKS):
            cut_s[j, pl.ds(t * feat_s.shape[1], feat_s.shape[1]), :] = feat_s[
                t, :, j * own_rows : (j + 1) * own_rows
            ]
    feat_own = pltpu.make_async_copy(cut_s.at[seq], feat_all.at[seq], load_sem.at[9])
    feat_own.start()

    def feat_copy(o):
        to = (seq + o) % n_dp
        return remote(
            cut_s.at[to], feat_all.at[seq], ft_send.at[o], ft_recv.at[o], {"dp": to}
        )

    for o in range(1, n_dp):
        feat_copy(o).start()

    loads["q"].wait()
    loads["k"].wait()
    loads["v"].wait()

    def stack(a, g):
        return jnp.concatenate(
            [a[:, (g * group + j) * HD : (g * group + j + 1) * HD] for j in range(group)], axis=0
        )

    rows_at = lax.rem(
        lax.broadcasted_iota(jnp.int32, (group * length, length), 0), jnp.int32(length)
    )
    cols_at = lax.broadcasted_iota(jnp.int32, (group * length, length), 1)
    causal = cols_at <= rows_at

    def softmax(t):
        for g in range(kv_local):
            kg = k_s[t, :, g * HD : (g + 1) * HD]
            scores = mul(stack(q_s[t], g), kg, LAST) * scale
            scores = jnp.where(causal, scores, -1e30)
            expo = jnp.exp(scores - jnp.max(scores, -1, keepdims=True))
            probs_s[t, g] = expo / jnp.sum(expo, -1, keepdims=True)

    for t in range(TICKS):
        softmax(t)

    def picks_second(t):
        @pl.when(section > 0)
        def _():
            remote(
                picks.at[seq, t], picks.at[seq, t], px_send.at[t, 0], px_recv.at[t],
                {"section": section},
            ).wait_recv()

        for o in range(1, n_dp):
            pick_copy(t, o).start()

    def pick_copy(t, o):
        to = (seq + o) % n_dp
        ref = picks.at[seq, t]
        return remote(ref, ref, pz_send.at[t, o], pz_recv.at[t, o], {"dp": to})

    def pick_spread(t, o):
        ref = picks.at[seq, t]
        return remote(ref, ref, px_send.at[t, o], px_recv.at[t], {"section": o})

    def rs_copy(t, i, where):
        return remote(
            send_s.at[t, i], recv_s.at[t, i], rs_send.at[t, i], rs_recv.at[t, i], {"mp": where}
        )

    def cross_copy(t, i, where):
        return remote(
            cross_s.at[t], cross_r.at[t, i], cr_send.at[t, i], cr_recv.at[t, i], {"mp": where}
        )

    part = length // pieces

    def held_copy(h):
        rows = pl.ds(h * part, part)
        return remote(
            out_s.at[0, rows], g_s.at[1, me, rows], held_send.at[h], held_recv.at[h],
            {"section": section - 1},
        )

    def finish_gather(t, rows_list):
        for h, rows in enumerate(rows_list):
            gather_forward(g_s.at[t], rows, ag_send.at[t, h], ag_recv.at[t, h])

    def tick(t):
        rows_list = [full] if t == 0 else [pl.ds(h * part, part) for h in range(pieces)]
        first = t == 0
        if t == 1:

            @pl.when(section == n_section - 1)
            def _():
                fresh_copy = pltpu.make_async_copy(
                    fresh.at[0, 0], g_s.at[1, me], load_sem.at[10]
                )
                fresh_copy.start()
                fresh_copy.wait()

            for h, rows in enumerate(rows_list):

                @pl.when(section < n_section - 1)
                def _():
                    held_copy(h).wait_recv()

                gather_start(g_s.at[1], rows, ag_send.at[1, h], ag_recv.at[1, h])
        if first:
            loads["wo0"].wait()
        d_attn = mul(g_s[t, me], wo_s[me], LAST)
        for h, rows in enumerate(rows_list):
            gather_wait(g_s.at[t], partner, 0, rows, ag_send.at[t, h], ag_recv.at[t, h])
        if first:
            loads["wo1"].wait()
        d_attn += mul(g_s[t, partner], wo_s[partner], LAST)
        finish_gather(t, rows_list)
        if first:
            loads["wo2"].wait()
        d_attn += mul(g_s[t, across], wo_s[across], LAST)
        for h, rows in enumerate(rows_list):
            gather_wait(g_s.at[t], diag, 2, rows, ag_send.at[t, h], ag_recv.at[t, h])
        if first:
            loads["wo3"].wait()
        d_attn += mul(g_s[t, diag], wo_s[diag], LAST)
        attn_s[...] = d_attn.astype(bf16)
        if first:
            gather_forward(x_s.at[0], x_rows[0], xg_send.at[0], xg_recv.at[0])
        else:
            picks_second(0)

        for g in range(kv_local):
            lanes = slice(g * HD, (g + 1) * HD)
            kg, vg = k_s[t, :, lanes], v_s[t, :, lanes]
            qg = stack(q_s[t], g)
            ag = stack(attn_s[...], g)
            probs = probs_s[t, g]
            d_probs = mul(ag, vg, LAST)
            inner = jnp.sum(probs * d_probs, -1, keepdims=True)
            d_scores = (probs * (d_probs - inner) * scale).astype(bf16)
            d_query = mul(d_scores, kg, PLAIN).astype(bf16)
            for j in range(group):
                dq_s[:, (g * group + j) * HD : (g * group + j + 1) * HD] = d_query[
                    j * length : (j + 1) * length
                ]
            dk_s[:, lanes] = mul(d_scores, qg, FIRST).astype(bf16)
            dv_s[:, lanes] = mul(probs.astype(bf16), ag, FIRST).astype(bf16)

        if first:
            gather_wait(x_s.at[0], partner, 0, x_rows[0], xg_send.at[0], xg_recv.at[0])
            gather_wait(x_s.at[0], diag, 2, x_rows[0], xg_send.at[0], xg_recv.at[0])
        else:
            gather_wait(x_s.at[1], partner, 0, x_rows[1], xg_send.at[1], xg_recv.at[1])
            gather_wait(x_s.at[1], diag, 2, x_rows[1], xg_send.at[1], xg_recv.at[1])

        def x_of(b):
            return x_s[t, b, pl.ds(0, length), :].astype(f32)

        def gain_of(b):
            return x_s[0, b, pl.ds(length, GAIN_ROWS), :].astype(f32)[0:1]

        def partial(i, b):
            if first:
                loads[f"wk{i}"].wait()
                loads[f"wv{i}"].wait()
                loads[f"wq{i}"].wait()
            term = mul(dq_s[...], wq_s[b], LAST)
            term += mul(dk_s[...], wk_s[b], LAST)
            return term + mul(dv_s[...], wv_s[b], LAST)

        term = partial(0, diag)
        send_s[t, 0] = term.astype(bf16)
        rs_copy(t, 0, partner).start()
        total = lane_sum(x_of(diag) * gain_of(diag) * term)
        term = partial(1, across)
        rs_copy(t, 0, partner).wait_recv()
        send_s[t, 1] = (term + recv_s[t, 0].astype(f32)).astype(bf16)
        rs_copy(t, 1, across).start()
        total += lane_sum(x_of(across) * gain_of(across) * term)
        term = partial(2, partner)
        send_s[t, 2] = term.astype(bf16)
        rs_copy(t, 2, partner).start()
        total += lane_sum(x_of(partner) * gain_of(partner) * term)
        term = partial(3, me)
        total += lane_sum(x_of(me) * gain_of(me) * term)
        padded = jnp.concatenate([total, jnp.zeros((LANES - length, LANES), f32)], axis=0)
        cross_s[t] = jnp.broadcast_to(
            jnp.sum(padded.T, axis=0, keepdims=True), cross_s.shape[1:]
        )
        for i, b in enumerate((partner, across, diag)):
            cross_copy(t, i, b).start()
        if first:
            gather_forward(x_s.at[1], x_rows[1], xg_send.at[1], xg_recv.at[1])
        squares = functools.reduce(
            lambda a, b: a + b, [lane_sum(x_of(b) * x_of(b)) for b in range(n_mp)]
        )
        squares = jnp.sum(squares, -1, keepdims=True)
        rstd = lax.rsqrt(squares / depth + 1e-05)
        rs_copy(t, 2, partner).wait_recv()
        term += recv_s[t, 2].astype(f32)
        rs_copy(t, 1, across).wait_recv()
        weighted = gain_of(me) * (term + recv_s[t, 1].astype(f32))
        cross = cross_s[t]
        for i in range(3):
            cross_copy(t, i, partner).wait_recv()
            cross += cross_r[t, i]
        cross = jnp.broadcast_to(cross[0:1], (LANES, LANES)).T[:length, 0:1]
        d_input = rstd * weighted - x_of(me) * (rstd * rstd * rstd) * (cross / depth)
        out_s[t] = (g_s[t, me].astype(f32) + d_input).astype(bf16)
        if first:

            @pl.when(section > 0)
            def _():
                for h in range(pieces):
                    held_copy(h).start()

            loads["pos"].wait()

        @pl.when(section == 0)
        def _():
            at = lax.broadcasted_iota(jnp.int32, (length, pos_s.shape[1]), 0)
            chosen = (at == pos_s[pl.ds(t, 1), :]).astype(f32).astype(bf16)
            picks[seq, t] = mul(chosen, out_s[t], FIRST).astype(bf16)
            for o in range(1, n_section):
                pick_spread(t, o).start()

    tick(0)
    tick(1)
    picks_second(1)
    pending[0, 0] = out_s[1]

    feat_own.wait()
    gather_drain(g_s.at[0], full, ag_send.at[0, 0], ag_recv.at[0, 0])
    for h in range(pieces):
        gather_drain(
            g_s.at[1], pl.ds(h * part, part), ag_send.at[1, h], ag_recv.at[1, h]
        )
    for t in range(TICKS):
        gather_drain(x_s.at[t], x_rows[t], xg_send.at[t], xg_recv.at[t])
        for i in range(3):
            rs_copy(t, i, partner).wait_send()
            cross_copy(t, i, partner).wait_send()

    @pl.when(section > 0)
    def _():
        for h in range(pieces):
            held_copy(h).wait_send()

    @pl.when(section == 0)
    def _():
        for t in range(TICKS):
            for o in range(1, n_section):
                pick_spread(t, o).wait_send()

    for o in range(1, n_dp):
        feat_copy(o).wait_send()
        source = (seq + n_dp - o) % n_dp
        remote(
            cut_s.at[seq], feat_all.at[source], ft_send.at[o], ft_recv.at[o], {"dp": source}
        ).wait_recv()
        for t in range(TICKS):
            pick_copy(t, o).wait_send()
            ref = picks.at[source, t]
            remote(ref, ref, pz_send.at[t, o], pz_recv.at[t, o], {"dp": source}).wait_recv()


def shards(
    w_query, w_key, w_value, w_out, norm_gain, saved_input, saved_query, saved_key,
    saved_value, grad_in, fresh_grad, features, image_pos, pieces=2,
):
    n_section, n_dp, n_mp = (lax.axis_size(a) for a in ("section", "dp", "mp"))
    assert n_mp == 4
    length, width = grad_in.shape[2:]
    kw = saved_key.shape[4]
    kv_local = kw // HD
    group = width // kw
    images = features.shape[2]
    own_rows = features.shape[3] // n_dp
    f32, bf16 = jnp.float32, jnp.bfloat16
    vmem, dma = pltpu.VMEM, pltpu.SemaphoreType.DMA
    feat_all, picks, pending = pl.pallas_call(
        functools.partial(kernel, n_section, n_dp, n_mp, pieces),
        out_shape=(
            jax.ShapeDtypeStruct((n_dp, TICKS * images, own_rows), bf16),
            jax.ShapeDtypeStruct((n_dp, TICKS, images, width), bf16),
            jax.ShapeDtypeStruct((1, 1, length, width), bf16),
        ),
        in_specs=[pl.BlockSpec(memory_space=pl.ANY)] * 13,
        out_specs=(pl.BlockSpec(memory_space=pltpu.VMEM),) * 3,
        scratch_shapes=[
            vmem((n_mp, width, width), bf16),
            vmem((n_mp, width, kw), bf16),
            vmem((n_mp, width, kw), bf16),
            vmem((n_mp, width, width), bf16),
            vmem((1, width), bf16),
            vmem((TICKS, n_mp, length + GAIN_ROWS, width), bf16),
            vmem((TICKS, length, width), bf16),
            vmem((TICKS, length, kw), bf16),
            vmem((TICKS, length, kw), bf16),
            vmem((TICKS, n_mp, length, width), bf16),
            vmem((TICKS, images, features.shape[3]), bf16),
            vmem((n_dp, TICKS * images, own_rows), bf16),
            vmem((TICKS, images), jnp.int32),
            vmem((TICKS, kv_local, group * length, length), f32),
            vmem((length, width), bf16),
            vmem((length, width), bf16),
            vmem((length, kw), bf16),
            vmem((length, kw), bf16),
            vmem((TICKS, length, width), bf16),
            vmem((TICKS, 3, length, width), bf16),
            vmem((TICKS, 3, length, width), bf16),
            vmem((TICKS, 8, LANES), f32),
            vmem((TICKS, 3, 8, LANES), f32),
            dma((11,)), dma((n_mp,)), dma((n_mp,)), dma((n_mp,)), dma((n_mp,)),
            dma((TICKS, pieces, 3)), dma((TICKS, pieces, 3)),
            dma((TICKS, 3)), dma((TICKS, 3)),
            dma((TICKS, 3)), dma((TICKS, 3)), dma((TICKS, 3)), dma((TICKS, 3)),
            dma((pieces,)), dma((pieces,)),
            dma((n_dp,)), dma((n_dp,)),
            dma((TICKS, n_section)), dma((TICKS,)),
            dma((TICKS, n_dp)), dma((TICKS, n_dp)),
        ],
        compiler_params=pltpu.CompilerParams(
            collective_id=0, has_side_effects=True, vmem_limit_bytes=48 * 2**20
        ),
    )(
        w_query, w_key, w_value, w_out, norm_gain, saved_input, saved_query, saved_key,
        saved_value, grad_in, fresh_grad, features, image_pos,
    )
    total = lax.dot_general(
        feat_all.reshape(-1, own_rows),
        picks.reshape(-1, width),
        FIRST,
        preferred_element_type=jnp.float32,
    )
    return total.astype(bf16), pending


def solution(mesh):
    in_specs = (
        P("section", None, "mp"),
        P("section", None, "mp"),
        P("section", None, "mp"),
        P("section", "mp", None),
        P("section", "mp"),
        P("section", None, "dp", None, "mp"),
        P("section", None, "dp", None, "mp"),
        P("section", None, "dp", None, "mp"),
        P("section", None, "dp", None, "mp"),
        P("section", "dp", None, "mp"),
        P(None, "dp", None, "mp"),
        P(None, "dp", None, "section"),
        P(None, "dp", None),
    )
    out_specs = (P(("section", "dp"), "mp"), P("section", "dp", None, "mp"))
    return jax.shard_map(shards, mesh=mesh, in_specs=in_specs, out_specs=out_specs, check_vma=False)
```

time: 176 us -> 62.8 us (0.36); the launches traced: 172 us -> 62.3 us
  waiting for transfers between devices: 48.6 us -> 0 us
  Pallas kernels: 0 us -> 48.2 us
  blocking collectives: 40.7 us -> 0 us
  matrix products: 37.1 us -> 1.97 us
  between operations: 14 us -> 0.66 us
  local copies, waits for them, and re-layouts: 20 us -> 11.5 us
  starting transfers between devices: 6.94 us -> 0 us
  other arithmetic: 5.13 us -> 0 us
    pallas_call x0 -> x1, Pallas kernels: none -> 48.2 us  [shards(): pl.pallas_call(functools.partial(kernel, n_section, n_dp, n_mp, pieces),...]
    dot_general x17 -> x1, matrix products: 35.8 us -> 1.97 us  [shards(): lax.dot_general(feat_all.reshape(-1, own_rows), picks.reshape(-1, width),...]
    reduce_scatter x2 -> x0, waiting for transfers between devices: 33.4 us -> none  [segment_step(): lax.psum_scatter(partial_term.astype(jnp.bfloat16), 'mp', scatter_dimensi...]
    all_gather x3 -> x0, blocking collectives: 28.8 us -> none  [the longest x1 14.5 us: shards(): lax.all_gather(image_grad[:, None], 'dp', axis=1, tiled=True)]
    psum x1 -> x0, waiting for transfers between devices: 13.5 us -> none  [spread_2(): return lax.psum(block, axis)]
    psum x2 -> x0, blocking collectives: 11.9 us -> none  [segment_step(): squares, cross = lax.psum((squares_local, cross_local), 'mp')]
    all_to_all x1 -> x0, starting transfers between devices: 4.6 us -> none  [shards(): lax.all_to_all(features, 'dp', split_axis=3, concat_axis=1, tiled=True)]
    all_to_all x1 -> x0, local copies, waits for them, and re-layouts: 4.47 us -> none  [shards(): lax.all_to_all(features, 'dp', split_axis=3, concat_axis=1, tiled=True)]
  transfers between devices with their start and end apart: 5 -> 0, of which waited for: 4 -> 0; matrix products, arithmetic and copies ran while one was open for 11% -> 0% of each run, Pallas kernels for 0% -> 0%
where the time goes in v1:
time: 62.8 us; the launch traced here: 62.3 us
  Pallas kernels  48.2 us (77%)
  local copies, waits for them, and re-layouts  11.5 us (18%)
  matrix products  1.97 us (3%)
  between operations  0.66 us (1%)
    pallas_call x1, Pallas kernels, shards(): pl.pallas_call(functools.partial(kernel, n_section, n_dp, n_mp, pieces),...  48.2 us
    unnamed x23, local copies, waits for them, and re-layouts  11.5 us
    dot_general x1, matrix products, shards(): lax.dot_general(feat_all.reshape(-1, own_rows), picks.reshape(-1, width),...  1.97 us

profile of v1, /device:TPU:2, one launch (start us, length us, event | category | flops | bytes accessed | tf_op | source)
XLA Modules:
  0.0 62.3 jit_solution(2514656118413360722)
XLA Ops:
  0.6 0.0 copy-start
  0.6 1.6 %copy-done = bf16[1,4096,256]{2,1,0:T(8,128)(2,1)S(1)} copy-done((bf16[1,4096,256]{2,1,0:T(8,128)(2,1)S(1)}, bf16[1,4096,256]{2,1,0:T(8,128)(2,1)}, u32[]{:S(2)}) %copy-start) | copy-done | bytes 2097176
  2.2 0.0 copy-start.1
  2.2 1.6 %copy-done.1 = bf16[1,4096,256]{2,1,0:T(8,128)(2,1)S(1)} copy-done((bf16[1,4096,256]{2,1,0:T(8,128)(2,1)S(1)}, bf16[1,4096,256]{2,1,0:T(8,128)(2,1)}, u32[]{:S(2)}) %copy-start.1) | copy-done | bytes 2097176
  3.8 0.0 copy-start.2
  3.8 0.9 %copy-done.2 = bf16[1,2,1,64,1024]{4,3,2,1,0:T(8,128)(2,1)S(1)} copy-done((bf16[1,2,1,64,1024]{4,3,2,1,0:T(8,128)(2,1)S(1)}, bf16[1,2,1,64,1024]{4,3,2,1,0:T(8,128)(2,1)}, u32[]{:S(2)}) %copy-start.2) | copy-done | bytes 262168
  4.8 0.0 copy-start.3
  4.8 0.9 %copy-done.3 = bf16[1,2,1,64,1024]{4,3,2,1,0:T(8,128)(2,1)S(1)} copy-done((bf16[1,2,1,64,1024]{4,3,2,1,0:T(8,128)(2,1)S(1)}, bf16[1,2,1,64,1024]{4,3,2,1,0:T(8,128)(2,1)}, u32[]{:S(2)}) %copy-start.3) | copy-done | bytes 262168
  5.7 0.0 copy-start.4
  5.7 0.9 %copy-done.4 = bf16[2,1,16,3840]{3,2,1,0:T(8,128)(2,1)S(1)} copy-done((bf16[2,1,16,3840]{3,2,1,0:T(8,128)(2,1)S(1)}, bf16[2,1,16,3840]{3,2,1,0:T(8,128)(2,1)}, u32[]{:S(2)}) %copy-start.4) | copy-done | bytes 245784
  6.7 0.0 copy-start.5
  6.7 0.9 %copy-done.5 = bf16[1,1,64,1024]{3,2,1,0:T(8,128)(2,1)S(1)} copy-done((bf16[1,1,64,1024]{3,2,1,0:T(8,128)(2,1)S(1)}, bf16[1,1,64,1024]{3,2,1,0:T(8,128)(2,1)}, u32[]{:S(2)}) %copy-start.5) | copy-done | bytes 131096
  7.6 0.0 copy-start.6
  7.6 0.9 %copy-done.6 = bf16[1,1,64,1024]{3,2,1,0:T(8,128)(2,1)S(1)} copy-done((bf16[1,1,64,1024]{3,2,1,0:T(8,128)(2,1)S(1)}, bf16[1,1,64,1024]{3,2,1,0:T(8,128)(2,1)}, u32[]{:S(2)}) %copy-start.6) | copy-done | bytes 131096
  8.5 0.0 copy-start.7
  8.5 0.8 %copy-done.7 = bf16[1,2,1,64,256]{4,3,2,1,0:T(8,128)(2,1)S(1)} copy-done((bf16[1,2,1,64,256]{4,3,2,1,0:T(8,128)(2,1)S(1)}, bf16[1,2,1,64,256]{4,3,2,1,0:T(8,128)(2,1)}, u32[]{:S(2)}) %copy-start.7) | copy-done | bytes 65560
  9.3 0.0 copy-start.8
  9.3 0.8 %copy-done.8 = bf16[1,2,1,64,256]{4,3,2,1,0:T(8,128)(2,1)S(1)} copy-done((bf16[1,2,1,64,256]{4,3,2,1,0:T(8,128)(2,1)S(1)}, bf16[1,2,1,64,256]{4,3,2,1,0:T(8,128)(2,1)}, u32[]{:S(2)}) %copy-start.8) | copy-done | bytes 65560
  10.2 0.0 copy-start.9
  10.2 0.7 %copy-done.9 = bf16[1,1024]{1,0:T(2,128)(2,1)S(1)} copy-done((bf16[1,1024]{1,0:T(2,128)(2,1)S(1)}, bf16[1,1024]{1,0:T(2,128)(2,1)}, u32[]{:S(2)}) %copy-start.9) | copy-done | bytes 2072
  10.8 0.0 copy-start.10
  10.8 0.7 %copy-done.10 = s32[2,1,16]{2,1,0:T(1,128)S(1)} copy-done((s32[2,1,16]{2,1,0:T(1,128)S(1)}, s32[2,1,16]{2,1,0:T(1,128)}, u32[]{:S(2)}) %copy-start.10) | copy-done | bytes 152
  11.5 48.2 %shard_map.140 = (bf16[4,32,960]{2,1,0:T(8,128)(2,1)S(1)}, bf16[4,2,16,1024]{3,2,1,0:T(8,128)(2,1)S(1)}, bf16[1,1,64,1024]{3,2,1,0:T(8,128)(2,1)S(1)}) custom-call(bf16[1,4096,1024]{2,1,0:T(8,128)(2,1)} %wq.1, bf16[1,4096,256]{2,1,0:T(8,128)(2,1)S(1)} %copy-done, bf16[1,4096,256]{2,1,0:T(8,128)(2,1)S(1)} %copy-done.1, bf16[1,1024,4096]{2,1,0:T(8,128)(2,1)} %wo.1, ...), custom_call_target="tpu_custom_call" | custom-call | tf_op jit(solution)/shard_map/pallas_call | solution.py:410
  59.7 2.0 %convolution_convert_fusion = bf16[960,1024]{1,0:T(8,128)(2,1)} fusion(bf16[128,960]{1,0:T(8,128)(2,1)S(1)} %bitcast.4, bf16[128,1024]{1,0:T(8,128)(2,1)S(1)} %bitcast.5), kind=kOutput, calls=%fused_computation | convolution fusion | flops 252641280 | bytes 2473984 | tf_op jit(solution)/shard_map/dot_general | solution.py:459
  61.7 0.7 %copy.16 = bf16[1,1,64,1024]{3,2,1,0:T(8,128)(2,1)} copy(bf16[1,1,64,1024]{3,2,1,0:T(8,128)(2,1)S(1)} %get-tuple-element.11) | data formatting | bytes 262144
Async XLA Ops:
  0.6 1.6 %copy-start = (bf16[1,4096,256]{2,1,0:T(8,128)(2,1)S(1)}, bf16[1,4096,256]{2,1,0:T(8,128)(2,1)}, u32[]{:S(2)}) copy-start(bf16[1,4096,256]{2,1,0:T(8,128)(2,1)} %wk.1) | copy-start | bytes 6291460
  2.2 1.6 %copy-start.1 = (bf16[1,4096,256]{2,1,0:T(8,128)(2,1)S(1)}, bf16[1,4096,256]{2,1,0:T(8,128)(2,1)}, u32[]{:S(2)}) copy-start(bf16[1,4096,256]{2,1,0:T(8,128)(2,1)} %wv.1) | copy-start | bytes 6291460
  3.8 0.9 %copy-start.2 = (bf16[1,2,1,64,1024]{4,3,2,1,0:T(8,128)(2,1)S(1)}, bf16[1,2,1,64,1024]{4,3,2,1,0:T(8,128)(2,1)}, u32[]{:S(2)}) copy-start(bf16[1,2,1,64,1024]{4,3,2,1,0:T(8,128)(2,1)} %x.1) | copy-start | bytes 786436
  4.8 0.9 %copy-start.3 = (bf16[1,2,1,64,1024]{4,3,2,1,0:T(8,128)(2,1)S(1)}, bf16[1,2,1,64,1024]{4,3,2,1,0:T(8,128)(2,1)}, u32[]{:S(2)}) copy-start(bf16[1,2,1,64,1024]{4,3,2,1,0:T(8,128)(2,1)} %q.1) | copy-start | bytes 786436
  5.7 0.9 %copy-start.4 = (bf16[2,1,16,3840]{3,2,1,0:T(8,128)(2,1)S(1)}, bf16[2,1,16,3840]{3,2,1,0:T(8,128)(2,1)}, u32[]{:S(2)}) copy-start(bf16[2,1,16,3840]{3,2,1,0:T(8,128)(2,1)} %feat.1) | copy-start | bytes 737284
  6.7 0.9 %copy-start.5 = (bf16[1,1,64,1024]{3,2,1,0:T(8,128)(2,1)S(1)}, bf16[1,1,64,1024]{3,2,1,0:T(8,128)(2,1)}, u32[]{:S(2)}) copy-start(bf16[1,1,64,1024]{3,2,1,0:T(8,128)(2,1)} %g_in.1) | copy-start | bytes 393220
  7.6 0.9 %copy-start.6 = (bf16[1,1,64,1024]{3,2,1,0:T(8,128)(2,1)S(1)}, bf16[1,1,64,1024]{3,2,1,0:T(8,128)(2,1)}, u32[]{:S(2)}) copy-start(bf16[1,1,64,1024]{3,2,1,0:T(8,128)(2,1)} %fresh.1) | copy-start | bytes 393220
  8.5 0.8 %copy-start.7 = (bf16[1,2,1,64,256]{4,3,2,1,0:T(8,128)(2,1)S(1)}, bf16[1,2,1,64,256]{4,3,2,1,0:T(8,128)(2,1)}, u32[]{:S(2)}) copy-start(bf16[1,2,1,64,256]{4,3,2,1,0:T(8,128)(2,1)} %k.1) | copy-start | bytes 196612
  9.3 0.8 %copy-start.8 = (bf16[1,2,1,64,256]{4,3,2,1,0:T(8,128)(2,1)S(1)}, bf16[1,2,1,64,256]{4,3,2,1,0:T(8,128)(2,1)}, u32[]{:S(2)}) copy-start(bf16[1,2,1,64,256]{4,3,2,1,0:T(8,128)(2,1)} %v.1) | copy-start | bytes 196612
  10.2 0.7 %copy-start.9 = (bf16[1,1024]{1,0:T(2,128)(2,1)S(1)}, bf16[1,1024]{1,0:T(2,128)(2,1)}, u32[]{:S(2)}) copy-start(bf16[1,1024]{1,0:T(2,128)(2,1)} %gain.1) | copy-start | bytes 6148
  10.8 0.7 %copy-start.10 = (s32[2,1,16]{2,1,0:T(1,128)S(1)}, s32[2,1,16]{2,1,0:T(1,128)}, u32[]{:S(2)}) copy-start(s32[2,1,16]{2,1,0:T(1,128)} %pos.1) | copy-start | bytes 388

commit v2 on v1

--- a/solution.py
+++ b/solution.py
@@ -27,11 +27,11 @@
 
 
 def kernel(
-    n_section, n_dp, n_mp, pieces,
+    n_section, n_dp, n_mp, pieces, halves,
     wq, wk, wv, wo, gain, x, q, k, v, g_in, fresh, feat, pos,
     feat_all, picks, pending,
     wq_s, wk_s, wv_s, wo_s, gain_s, x_s, q_s, k_s, v_s, g_s, feat_s, cut_s, pos_s,
-    probs_s, attn_s, dq_s, dk_s, dv_s, out_s, send_s, recv_s, cross_s, cross_r,
+    probs_s, attn_s, dq_s, dk_s, dv_s, out_s, send_s, recv_s, term_s, cross_s, cross_r,
     load_sem, wo_sem, wq_sem, wk_sem, wv_sem,
     ag_send, ag_recv, xg_send, xg_recv, rs_send, rs_recv, cr_send, cr_recv,
     held_send, held_recv, ft_send, ft_recv, px_send, px_recv, pz_send, pz_recv,
@@ -192,9 +192,13 @@
         ref = picks.at[seq, t]
         return remote(ref, ref, px_send.at[t, o], px_recv.at[t], {"section": o})
 
-    def rs_copy(t, i, where):
+    block = width // halves
+
+    def rs_copy(t, i, h, where):
+        lanes = pl.ds(h * block, block)
         return remote(
-            send_s.at[t, i], recv_s.at[t, i], rs_send.at[t, i], rs_recv.at[t, i], {"mp": where}
+            send_s.at[t, i, :, lanes], recv_s.at[t, i, :, lanes],
+            rs_send.at[t, i, h], rs_recv.at[t, i, h], {"mp": where},
         )
 
     def cross_copy(t, i, where):
@@ -253,9 +257,7 @@
             loads["wo3"].wait()
         d_attn += mul(g_s[t, diag], wo_s[diag], LAST)
         attn_s[...] = d_attn.astype(bf16)
-        if first:
-            gather_forward(x_s.at[0], x_rows[0], xg_send.at[0], xg_recv.at[0])
-        else:
+        if not first:
             picks_second(0)
 
         for g in range(kv_local):
@@ -275,43 +277,47 @@
             dk_s[:, lanes] = mul(d_scores, qg, FIRST).astype(bf16)
             dv_s[:, lanes] = mul(probs.astype(bf16), ag, FIRST).astype(bf16)
 
-        if first:
-            gather_wait(x_s.at[0], partner, 0, x_rows[0], xg_send.at[0], xg_recv.at[0])
-            gather_wait(x_s.at[0], diag, 2, x_rows[0], xg_send.at[0], xg_recv.at[0])
-        else:
-            gather_wait(x_s.at[1], partner, 0, x_rows[1], xg_send.at[1], xg_recv.at[1])
-            gather_wait(x_s.at[1], diag, 2, x_rows[1], xg_send.at[1], xg_recv.at[1])
-
         def x_of(b):
             return x_s[t, b, pl.ds(0, length), :].astype(f32)
 
         def gain_of(b):
             return x_s[0, b, pl.ds(length, GAIN_ROWS), :].astype(f32)[0:1]
 
-        def partial(i, b):
-            if first:
+        def partial(i, b, h):
+            if first and h == 0:
                 loads[f"wk{i}"].wait()
                 loads[f"wv{i}"].wait()
                 loads[f"wq{i}"].wait()
-            term = mul(dq_s[...], wq_s[b], LAST)
-            term += mul(dk_s[...], wk_s[b], LAST)
-            return term + mul(dv_s[...], wv_s[b], LAST)
-
-        term = partial(0, diag)
-        send_s[t, 0] = term.astype(bf16)
-        rs_copy(t, 0, partner).start()
-        total = lane_sum(x_of(diag) * gain_of(diag) * term)
-        term = partial(1, across)
-        rs_copy(t, 0, partner).wait_recv()
-        send_s[t, 1] = (term + recv_s[t, 0].astype(f32)).astype(bf16)
-        rs_copy(t, 1, across).start()
-        total += lane_sum(x_of(across) * gain_of(across) * term)
-        term = partial(2, partner)
-        send_s[t, 2] = term.astype(bf16)
-        rs_copy(t, 2, partner).start()
-        total += lane_sum(x_of(partner) * gain_of(partner) * term)
-        term = partial(3, me)
-        total += lane_sum(x_of(me) * gain_of(me) * term)
+            at = slice(h * block, (h + 1) * block)
+            term = mul(dq_s[...], wq_s[b, at], LAST)
+            term += mul(dk_s[...], wk_s[b, at], LAST)
+            term += mul(dv_s[...], wv_s[b, at], LAST)
+            term_s[i, :, at] = term
+            return at, term
+
+        for h in range(halves):
+            at, term = partial(0, diag, h)
+            send_s[t, 0, :, at] = term.astype(bf16)
+            rs_copy(t, 0, h, partner).start()
+        for h in range(halves):
+            at, term = partial(1, across, h)
+            rs_copy(t, 0, h, partner).wait_recv()
+            send_s[t, 1, :, at] = (term + recv_s[t, 0, :, at].astype(f32)).astype(bf16)
+            rs_copy(t, 1, h, across).start()
+        for h in range(halves):
+            at, term = partial(2, partner, h)
+            send_s[t, 2, :, at] = term.astype(bf16)
+            rs_copy(t, 2, h, partner).start()
+        if first:
+            gather_forward(x_s.at[0], x_rows[0], xg_send.at[0], xg_recv.at[0])
+        for h in range(halves):
+            partial(3, me, h)
+        gather_wait(x_s.at[t], partner, 0, x_rows[t], xg_send.at[t], xg_recv.at[t])
+        total = jnp.zeros((length, LANES), f32)
+        for i, b in ((1, across), (2, partner), (3, me), (0, diag)):
+            if i == 0:
+                gather_wait(x_s.at[t], diag, 2, x_rows[t], xg_send.at[t], xg_recv.at[t])
+            total += lane_sum(x_of(b) * gain_of(b) * term_s[i])
         padded = jnp.concatenate([total, jnp.zeros((LANES - length, LANES), f32)], axis=0)
         cross_s[t] = jnp.broadcast_to(
             jnp.sum(padded.T, axis=0, keepdims=True), cross_s.shape[1:]
@@ -325,24 +331,31 @@
         )
         squares = jnp.sum(squares, -1, keepdims=True)
         rstd = lax.rsqrt(squares / depth + 1e-05)
-        rs_copy(t, 2, partner).wait_recv()
-        term += recv_s[t, 2].astype(f32)
-        rs_copy(t, 1, across).wait_recv()
-        weighted = gain_of(me) * (term + recv_s[t, 1].astype(f32))
+        for h in range(halves):
+            rs_copy(t, 2, h, partner).wait_recv()
+        for h in range(halves):
+            rs_copy(t, 1, h, across).wait_recv()
         cross = cross_s[t]
         for i in range(3):
             cross_copy(t, i, partner).wait_recv()
             cross += cross_r[t, i]
         cross = jnp.broadcast_to(cross[0:1], (LANES, LANES)).T[:length, 0:1]
-        d_input = rstd * weighted - x_of(me) * (rstd * rstd * rstd) * (cross / depth)
-        out_s[t] = (g_s[t, me].astype(f32) + d_input).astype(bf16)
-        if first:
-
-            @pl.when(section > 0)
-            def _():
-                for h in range(pieces):
+        factor = rstd * rstd * rstd * (cross / depth)
+        for h in range(pieces if first else 1):
+            rows = slice(h * part, (h + 1) * part) if first else slice(0, length)
+            d_normed = (
+                term_s[3, rows] + recv_s[t, 2, rows].astype(f32) + recv_s[t, 1, rows].astype(f32)
+            )
+            own = x_s[t, me, rows].astype(f32)
+            d_input = rstd[rows] * (gain_of(me) * d_normed) - own * factor[rows]
+            out_s[t, rows] = (g_s[t, me, rows].astype(f32) + d_input).astype(bf16)
+            if first:
+
+                @pl.when(section > 0)
+                def _():
                     held_copy(h).start()
 
+        if first:
             loads["pos"].wait()
 
         @pl.when(section == 0)
@@ -367,7 +380,8 @@
     for t in range(TICKS):
         gather_drain(x_s.at[t], x_rows[t], xg_send.at[t], xg_recv.at[t])
         for i in range(3):
-            rs_copy(t, i, partner).wait_send()
+            for h in range(halves):
+                rs_copy(t, i, h, partner).wait_send()
             cross_copy(t, i, partner).wait_send()
 
     @pl.when(section > 0)
@@ -395,7 +409,7 @@
 
 def shards(
     w_query, w_key, w_value, w_out, norm_gain, saved_input, saved_query, saved_key,
-    saved_value, grad_in, fresh_grad, features, image_pos, pieces=2,
+    saved_value, grad_in, fresh_grad, features, image_pos, pieces=4, halves=1,
 ):
     n_section, n_dp, n_mp = (lax.axis_size(a) for a in ("section", "dp", "mp"))
     assert n_mp == 4
@@ -408,13 +422,13 @@
     f32, bf16 = jnp.float32, jnp.bfloat16
     vmem, dma = pltpu.VMEM, pltpu.SemaphoreType.DMA
     feat_all, picks, pending = pl.pallas_call(
-        functools.partial(kernel, n_section, n_dp, n_mp, pieces),
+        functools.partial(kernel, n_section, n_dp, n_mp, pieces, halves),
         out_shape=(
             jax.ShapeDtypeStruct((n_dp, TICKS * images, own_rows), bf16),
             jax.ShapeDtypeStruct((n_dp, TICKS, images, width), bf16),
             jax.ShapeDtypeStruct((1, 1, length, width), bf16),
         ),
-        in_specs=[pl.BlockSpec(memory_space=pl.ANY)] * 13,
+        in_specs=[pl.BlockSpec(memory_space=pltpu.HBM)] * 13,
         out_specs=(pl.BlockSpec(memory_space=pltpu.VMEM),) * 3,
         scratch_shapes=[
             vmem((n_mp, width, width), bf16),
@@ -438,12 +452,13 @@
             vmem((TICKS, length, width), bf16),
             vmem((TICKS, 3, length, width), bf16),
             vmem((TICKS, 3, length, width), bf16),
+            vmem((n_mp, length, width), f32),
             vmem((TICKS, 8, LANES), f32),
             vmem((TICKS, 3, 8, LANES), f32),
             dma((11,)), dma((n_mp,)), dma((n_mp,)), dma((n_mp,)), dma((n_mp,)),
             dma((TICKS, pieces, 3)), dma((TICKS, pieces, 3)),
             dma((TICKS, 3)), dma((TICKS, 3)),
-            dma((TICKS, 3)), dma((TICKS, 3)), dma((TICKS, 3)), dma((TICKS, 3)),
+            dma((TICKS, 3, halves)), dma((TICKS, 3, halves)), dma((TICKS, 3)), dma((TICKS, 3)),
             dma((pieces,)), dma((pieces,)),
             dma((n_dp,)), dma((n_dp,)),
             dma((TICKS, n_section)), dma((TICKS,)),
@@ -453,8 +468,13 @@
             collective_id=0, has_side_effects=True, vmem_limit_bytes=48 * 2**20
         ),
     )(
-        w_query, w_key, w_value, w_out, norm_gain, saved_input, saved_query, saved_key,
-        saved_value, grad_in, fresh_grad, features, image_pos,
+        *[
+            pltpu.with_memory_space_constraint(a, pltpu.HBM)
+            for a in (
+                w_query, w_key, w_value, w_out, norm_gain, saved_input, saved_query, saved_key,
+                saved_value, grad_in, fresh_grad, features, image_pos,
+            )
+        ]
     )
     total = lax.dot_general(
         feat_all.reshape(-1, own_rows),

time: 62.8 us -> 47.6 us (0.76)
  local copies, waits for them, and re-layouts: 11.5 us -> 0.65 us
  Pallas kernels: 48.2 us -> 44.2 us
    unnamed x23 -> x1, local copies, waits for them, and re-layouts: 11.5 us -> 0.65 us
    pallas_call x1, Pallas kernels: 48.2 us -> 44.2 us  [shards(): pl.pallas_call(functools.partial(kernel, n_section, n_dp, n_mp, pieces, h...]
where the time goes in v2:
time: 47.6 us; the launch traced here: 47.5 us
  Pallas kernels  44.2 us (93%)
  matrix products  1.97 us (4%)
  local copies, waits for them, and re-layouts  0.65 us (1%)
  between operations  0.64 us (1%)
    pallas_call x1, Pallas kernels, shards(): pl.pallas_call(functools.partial(kernel, n_section, n_dp, n_mp, pieces, h...  44.2 us
    dot_general x1, matrix products, shards(): lax.dot_general(feat_all.reshape(-1, own_rows), picks.reshape(-1, width),...  1.97 us

profile of v2, /device:TPU:2, one launch (start us, length us, event | category | flops | bytes accessed | tf_op | source)
XLA Modules:
  0.0 47.5 jit_solution(13723726633727619202)
XLA Ops:
  0.6 44.2 %shard_map.140 = (bf16[4,32,960]{2,1,0:T(8,128)(2,1)S(1)}, bf16[4,2,16,1024]{3,2,1,0:T(8,128)(2,1)S(1)}, bf16[1,1,64,1024]{3,2,1,0:T(8,128)(2,1)S(1)}) custom-call(bf16[1,4096,1024]{2,1,0:T(8,128)(2,1)} %wq.1, bf16[1,4096,256]{2,1,0:T(8,128)(2,1)} %wk.1, bf16[1,4096,256]{2,1,0:T(8,128)(2,1)} %wv.1, bf16[1,1024,4096]{2,1,0:T(8,128)(2,1)} %wo.1, ...), custom_call_target="tpu_custom_call" | custom-call | tf_op jit(solution)/shard_map/pallas_call | solution.py:424
  44.9 2.0 %convolution_convert_fusion = bf16[960,1024]{1,0:T(8,128)(2,1)} fusion(bf16[128,960]{1,0:T(8,128)(2,1)S(1)} %bitcast.4, bf16[128,1024]{1,0:T(8,128)(2,1)S(1)} %bitcast.5), kind=kOutput, calls=%fused_computation | convolution fusion | flops 252641280 | bytes 2473984 | tf_op jit(solution)/shard_map/dot_general | solution.py:479
  46.8 0.7 %copy.16 = bf16[1,1,64,1024]{3,2,1,0:T(8,128)(2,1)} copy(bf16[1,1,64,1024]{3,2,1,0:T(8,128)(2,1)S(1)} %get-tuple-element.11) | data formatting | bytes 262144
